TPU v7x, 32 devices: a whole 2x2x4 slice. The times are simulated.
32 devices in a mesh: group: 2 (over x), row: 16 (over z, y, core).
Axes of the slice: x: 2, y: 2, z: 4, core: 2. Of those that a mesh axis runs over, the one named last changes fastest.
Arguments:
- alignment: bfloat16 [256, 128, 256], P(('group', 'row')), parts along dimension 0, may hold values from -6 to 6
- pair_rep: bfloat16 [256, 128, 128], P(('group', 'row')), parts along dimension 0, may hold values from -6 to 6
- alignment_norm_gain: float32 [256], replicated, may hold values from 0.5 to 1.5
- alignment_norm_offset: float32 [256], replicated, may hold values from -3 to 3
- left_projection_weight: bfloat16 [256, 32], replicated, may hold values from -0.375 to 0.375
- right_projection_weight: bfloat16 [256, 32], replicated, may hold values from -0.375 to 0.375
- outer_weight: bfloat16 [1024, 128], replicated, may hold values from -0.75 to 0.75
- outer_bias: float32 [128], replicated, may hold values from -3 to 3
- pair_gain: float32 [128], replicated, may hold values from 0.5 to 1.5
- pair_shift: float32 [128], replicated, may hold values from -3 to 3
- up_weight: bfloat16 [128, 512], replicated, may hold values from -0.5 to 0.5
- up_bias: float32 [512], replicated, may hold values from -3 to 3
- down_weight: bfloat16 [512, 128], replicated, may hold values from -0.25 to 0.25
- down_bias: float32 [128], replicated, may hold values from -3 to 3
Outputs:
- pair_out: bfloat16 [256, 128, 128], P(('group', 'row')), parts along dimension 0
There are 2 independent parts, one for each index of `group`. A program takes and returns all parts, laid end to end along the dimension named above; an argument that names none is the same for every part. Nothing has to cross between parts.
All inputs are finite; a program needn't handle non-finite values.
Results may differ from a plain program's by a relative error of at most 0.005.
Values may be sent and summed in bfloat16 or wider, within the bound.
A program may use at most 128 MiB of HBM per device.

v0:
```python
import jax
import jax.numpy as jnp
from jax import lax
from jax.sharding import PartitionSpec as P

epsilon = 1e-05


def layer_norm(values, gain, shift):
    values = values.astype(jnp.float32)
    center = jnp.mean(values, axis=-1, keepdims=True)
    spread = jnp.mean(jnp.square(values - center), axis=-1, keepdims=True)
    return (values - center) * lax.rsqrt(spread + epsilon) * gain + shift


def project_both(normed, left_projection_weight, right_projection_weight):
    left = jnp.einsum(
        "src,cd->rsd", normed, left_projection_weight, preferred_element_type=jnp.float32
    ).astype(jnp.bfloat16)
    right = jnp.einsum(
        "src,cd->rsd", normed, right_projection_weight, preferred_element_type=jnp.float32
    ).astype(jnp.bfloat16)
    return (left, right)


def pair_update(left_flat, right_flat, pair_tile, layer_params, proj_w):
    outer_weight, outer_bias, pair_gain, pair_shift, up_weight, up_bias, down_weight, down_bias = (
        layer_params
    )
    rows_i = left_flat.shape[0]
    rows_j = right_flat.shape[0]
    width = outer_weight.shape[1]
    seq_total = left_flat.shape[1] // proj_w
    left_rows = left_flat.reshape(rows_i, seq_total, proj_w)
    right_rows = right_flat.reshape(rows_j, seq_total, proj_w)
    outer_mean = jnp.einsum(
        "isc,jse->ijce", left_rows, right_rows, preferred_element_type=jnp.float32
    ) * (1.0 / seq_total)
    outer_mean = outer_mean.astype(jnp.bfloat16).reshape(rows_i * rows_j, proj_w * proj_w)
    summed = (
        pair_tile.reshape(rows_i * rows_j, width).astype(jnp.float32)
        + jnp.dot(outer_mean, outer_weight, preferred_element_type=jnp.float32)
        + outer_bias
    )
    normed = layer_norm(summed, pair_gain, pair_shift).astype(jnp.bfloat16)
    hidden = jax.nn.relu(
        jnp.dot(normed, up_weight, preferred_element_type=jnp.float32) + up_bias
    ).astype(jnp.bfloat16)
    result = summed + jnp.dot(hidden, down_weight, preferred_element_type=jnp.float32) + down_bias
    return result.astype(jnp.bfloat16).reshape(rows_i, rows_j, width)


def in_blocks(amount, builder):
    if amount > 256 and amount % 256 == 0:
        stacked = lax.map(
            lambda which_k: builder(which_k * 256, 256), jnp.arange(amount // 256, dtype=jnp.int32)
        )
        return stacked.reshape((amount,) + stacked.shape[2:])
    return builder(0, amount)


def shards(
    alignment,
    pair_rep,
    alignment_norm_gain,
    alignment_norm_offset,
    left_projection_weight,
    right_projection_weight,
    outer_weight,
    outer_bias,
    pair_gain,
    pair_shift,
    up_weight,
    up_bias,
    down_weight,
    down_bias,
):
    proj_w = left_projection_weight.shape[1]
    normed = layer_norm(alignment, alignment_norm_gain, alignment_norm_offset).astype(jnp.bfloat16)
    left, right = project_both(normed, left_projection_weight, right_projection_weight)
    left, right = (
        lax.all_to_all(left, "row", split_axis=0, concat_axis=1, tiled=True),
        lax.all_to_all(right, "row", split_axis=0, concat_axis=1, tiled=True),
    )
    left = left.reshape(left.shape[0], -1)
    right = right.reshape(right.shape[0], -1)
    layer_params = (
        outer_weight,
        outer_bias,
        pair_gain,
        pair_shift,
        up_weight,
        up_bias,
        down_weight,
        down_bias,
    )
    pieces = lax.all_gather(right, "row", axis=0, tiled=True)
    offset = jnp.int32(0)

    def builder(inner_start, amount):
        segment = lax.dynamic_slice_in_dim(pieces, inner_start, amount, 0)
        pair_tile = lax.dynamic_slice_in_dim(pair_rep, offset + inner_start, amount, 1)
        return jnp.transpose(pair_update(left, segment, pair_tile, layer_params, proj_w), (1, 0, 2))

    columns = in_blocks(pieces.shape[0], builder)
    return lax.all_to_all(columns, "row", split_axis=0, concat_axis=1, tiled=True)


def solution(mesh):
    placed = (
        P(("group", "row"), None, None),
        P(("group", "row"), None, None),
        P(),
        P(),
        P(),
        P(),
        P(),
        P(),
        P(),
        P(),
        P(),
        P(),
        P(),
        P(),
    )
    return jax.shard_map(
        shards,
        mesh=mesh,
        in_specs=placed,
        out_specs=P(("group", "row"), None, None),
        check_vma=False,
    )
```

profile of v0, /device:TPU:0, one launch (start us, length us, event | category | flops | bytes accessed | tf_op | source)
XLA Modules:
  0.0 88.8 jit_solution(10173570081271924435)
XLA Ops:
  6.5 0.0 copy-start
  6.5 0.0 all-gather.2.cloned.1.call-start
  6.5 1.3 %convert_reduce_fusion = f32[8,128]{1,0:T(8,128)S(1)} fusion(bf16[8,128,256]{2,1,0:T(8,128)(2,1)} %param.14), kind=kLoop, calls=%fused_computation.8 | loop fusion | flops 523264 | bytes 528384 | tf_op jit(solution)/shard_map/reduce_sum | solution.py:11
  7.8 0.0 copy-start.1
  7.9 0.0 copy-start.5
  7.9 0.0 copy-start.7
  7.9 0.0 copy-start.8
  7.9 1.5 %fusion.18 = f32[8,128]{1,0:T(8,128)S(1)} fusion(bf16[8,128,256]{2,1,0:T(8,128)(2,1)} %param.14, f32[8,128]{1,0:T(8,128)S(1)} %broadcast_multiply_fusion.1), kind=kLoop, calls=%fused_computation.20 | loop fusion | flops 1047552 | bytes 532480 | tf_op jit(solution)/shard_map/reduce_sum | solution.py:12
  9.4 1.5 %fusion.16 = bf16[128,8,32]{0,2,1:T(8,128)(2,1)S(1)} fusion(bf16[8,128,256]{2,1,0:T(8,128)(2,1)} %param.14, f32[256]{0:T(256)} %param.17, f32[256]{0:T(256)} %param.16, f32[8,128]{1,0:T(8,128)S(1)} %add_rsqrt_fusion.1, f32[8,128]{1,0:T(8,128)S(1)} %broadcast_multiply_fusion.1, bf16[256,32]{0,1:T(8,128)(2,1)} %param.19), kind=kOutput, calls=%fused_computation.18 | convolution fusion | flops 18382848 | bytes 616448 | tf_op jit(solution)/shard_map/src,cd->rsd/dot_general | solution.py:20
  10.9 0.2 copy.26
  11.1 0.3 reshape.56
  11.4 14.1 %all_to_all.51 = bf16[16,2,1024]{2,1,0:T(2,128)(2,1)S(1)} all-to-all(bf16[16,2,1024]{2,1,0:T(2,128)(2,1)S(1)} %reshape.56), channel_id=1, replica_groups=mesh['group'=2,'row'=16] {'row'}, dimensions={0} | all-to-all | bytes 131072 | tf_op jit(solution)/shard_map/all_to_all | solution.py:83
  25.5 0.2 reshape.57
  25.8 0.9 %reshape.47 = bf16[8,4096]{1,0:T(8,128)(2,1)} reshape(bf16[8,16,8,32]{3,2,1,0:T(8,128)(2,1)S(1)} %copy.27) | data formatting | bytes 131072 | tf_op jit(solution)/shard_map/reshape | solution.py:86
  26.7 0.0 all-gather.2.cloned.1.call-update
  26.7 0.0 copy-done.1
  26.7 0.0 copy-done.5
  26.7 0.0 copy-done.7
  26.7 0.0 copy-done.8
  26.7 0.5 fusion.17
  27.2 0.2 copy.29
  27.4 0.3 reshape.58
  27.7 9.5 %all_to_all.52 = bf16[16,2,1024]{2,1,0:T(2,128)(2,1)S(1)} all-to-all(bf16[16,2,1024]{2,1,0:T(2,128)(2,1)S(1)} %reshape.58), channel_id=1, replica_groups=mesh['group'=2,'row'=16] {'row'}, dimensions={0} | all-to-all | bytes 131072 | tf_op jit(solution)/shard_map/all_to_all | solution.py:82
  37.2 0.2 reshape.59
  37.3 24.7 %all-gather.2.cloned.1.call-done = bf16[128,4096]{1,0:T(8,128)(2,1)} async-done(((bf16[8,4096]{1,0:T(8,128)(2,1)}), bf16[128,4096]{1,0:T(8,128)(2,1)}) %all-gather.2.cloned.1.call-update) | async-done | bytes 1048592 | tf_op jit(solution)/shard_map/all_gather | solution.py:97
  62.0 1.6 %copy.28 = bf16[128,4096]{0,1:T(8,128)(2,1)S(1)} copy(bf16[128,4096]{1,0:T(8,128)(2,1)} %all-gather.2.cloned.1.call-done) | data formatting | bytes 2097152 | tf_op jit(solution)/shard_map/all_gather | solution.py:97
  63.6 0.8 fusion.3
  64.4 0.0 copy-start.2
  64.5 0.0 copy-start.9
  64.5 0.8 copy.33
  65.3 0.0 copy-done
  65.3 0.1 copy-done.2
  65.4 0.0 copy-done.9
  65.4 0.0 copy-start.3
  65.4 0.0 copy-start.4
  65.4 0.0 copy-start.6
  65.4 0.0 copy-start.10
  65.4 0.0 copy-start.11
  65.4 0.0 copy-start.12
  65.4 0.8 fusion.40
  66.3 0.4 multiply_reduce_fusion
  66.7 0.0 copy-done.3
  66.7 0.0 copy-done.4
  66.7 0.0 copy-done.6
  66.7 0.0 copy-done.10
  66.7 0.0 copy-done.11
  66.7 0.0 copy-done.12
  66.7 0.8 fusion.15
  67.5 0.2 copy.61
  67.7 13.5 %all_to_all.53 = bf16[128,8,128]{2,1,0:T(8,128)(2,1)S(1)} all-to-all(bf16[128,8,128]{2,1,0:T(8,128)(2,1)S(1)} %bitcast.59), channel_id=1, replica_groups=mesh['group'=2,'row'=16] {'row'}, dimensions={0} | all-to-all | bytes 524288 | tf_op jit(solution)/shard_map/all_to_all | solution.py:106
  81.2 0.8 copy.60
  (5 shorter events, 0.1 us)
Async XLA Ops:
  6.5 58.7 %copy-start = (bf16[1024,128]{1,0:T(8,128)(2,1)S(1)}, bf16[1024,128]{1,0:T(8,128)(2,1)}, u32[]{:S(2)}) copy-start(bf16[1024,128]{1,0:T(8,128)(2,1)} %param.20) | copy-start | bytes 786436
  6.5 55.5 %all-gather.2.cloned.1.call-start = ((), (), s32[]{:S(2)}) async-start(), calls=%async_computation.3 | async-start | bytes 1114112 | tf_op jit(solution)/shard_map/all_gather | solution.py:97
  7.8 18.9 %copy-start.1 = (bf16[8,128,256]{2,1,0:T(8,128)(2,1)S(1)}, bf16[8,128,256]{2,1,0:T(8,128)(2,1)}, u32[]{:S(2)}) copy-start(bf16[8,128,256]{2,1,0:T(8,128)(2,1)} %param.14) | copy-start | bytes 1572868
  7.9 18.8 %copy-start.5 = (bf16[256,32]{0,1:T(8,128)(2,1)S(1)}, bf16[256,32]{0,1:T(8,128)(2,1)}, u32[]{:S(2)}) copy-start(bf16[256,32]{0,1:T(8,128)(2,1)} %param.18) | copy-start | bytes 49156
  7.9 18.8 %copy-start.7 = (f32[256]{0:T(256)S(1)}, f32[256]{0:T(256)}, u32[]{:S(2)}) copy-start(f32[256]{0:T(256)} %param.17) | copy-start | bytes 3076
  7.9 18.8 %copy-start.8 = (f32[256]{0:T(256)S(1)}, f32[256]{0:T(256)}, u32[]{:S(2)}) copy-start(f32[256]{0:T(256)} %param.16) | copy-start | bytes 3076
  64.4 1.0 %copy-start.2 = (bf16[8,128,128]{2,1,0:T(8,128)(2,1)S(1)}, bf16[8,128,128]{2,1,0:T(8,128)(2,1)}, u32[]{:S(2)}) copy-start(bf16[8,128,128]{2,1,0:T(8,128)(2,1)} %param.15) | copy-start | bytes 786436
  64.5 0.9 %copy-start.9 = (f32[128]{0:T(128)S(1)}, f32[128]{0:T(128)}, u32[]{:S(2)}) copy-start(f32[128]{0:T(128)} %param.21) | copy-start | bytes 1540
  65.4 1.3 %copy-start.3 = (bf16[512,128]{1,0:T(8,128)(2,1)S(1)}, bf16[512,128]{1,0:T(8,128)(2,1)}, u32[]{:S(2)}) copy-start(bf16[512,128]{1,0:T(8,128)(2,1)} %param.26) | copy-start | bytes 393220
  65.4 1.3 %copy-start.4 = (bf16[128,512]{1,0:T(8,128)(2,1)S(1)}, bf16[128,512]{1,0:T(8,128)(2,1)}, u32[]{:S(2)}) copy-start(bf16[128,512]{1,0:T(8,128)(2,1)} %param.24) | copy-start | bytes 393220
  65.4 1.3 %copy-start.6 = (f32[512]{0:T(512)S(1)}, f32[512]{0:T(512)}, u32[]{:S(2)}) copy-start(f32[512]{0:T(512)} %param.25) | copy-start | bytes 6148
  65.4 1.3 %copy-start.10 = (f32[128]{0:T(128)S(1)}, f32[128]{0:T(128)}, u32[]{:S(2)}) copy-start(f32[128]{0:T(128)} %param.27) | copy-start | bytes 1540
  65.4 1.3 %copy-start.11 = (f32[128]{0:T(128)S(1)}, f32[128]{0:T(128)}, u32[]{:S(2)}) copy-start(f32[128]{0:T(128)} %param.23) | copy-start | bytes 1540
  65.4 1.3 %copy-start.12 = (f32[128]{0:T(128)S(1)}, f32[128]{0:T(128)}, u32[]{:S(2)}) copy-start(f32[128]{0:T(128)} %param.22) | copy-start | bytes 1540
Sparse Core Ops, SparseCore 0:
  26.8 35.1 all-gather.1
where the time goes:
time: 89.1 us; the launch traced here: 88.8 us
  blocking collectives  37.1 us (42%)
  waiting for transfers between devices  24.7 us (28%)
  between operations  13.7 us (15%)
  local copies, waits for them, and re-layouts  5.79 us (6%)
  matrix products  4.41 us (5%)
  other arithmetic  3.14 us (4%)
    all_gather x1, waiting for transfers between devices, shards(): pieces = lax.all_gather(right, 'row', axis=0, tiled=True)  24.7 us
    all_to_all x1, blocking collectives, shards(): lax.all_to_all(right, 'row', split_axis=0, concat_axis=1, tiled=True)  14.1 us
    all_to_all x1, blocking collectives, shards(): lax.all_to_all(columns, 'row', split_axis=0, concat_axis=1, tiled=True)  13.5 us
    all_to_all x1, blocking collectives, shards(): lax.all_to_all(left, 'row', split_axis=0, concat_axis=1, tiled=True)  9.48 us
    reduce_sum x2, other arithmetic, layer_norm(): spread = jnp.mean(jnp.square(values - center), axis=-1, keepdims=True)  1.83 us
  transfers between devices with their start and end apart: 1, of which 1 were waited for; matrix products, arithmetic and copies ran while one was open for 1% of the time, Pallas kernels for 0%

commit v1 on v0

--- a/solution.py
+++ b/solution.py
@@ -1,9 +1,14 @@
+import functools
+
 import jax
 import jax.numpy as jnp
 from jax import lax
+from jax.experimental import pallas as pl
+from jax.experimental.pallas import tpu as pltpu
 from jax.sharding import PartitionSpec as P
 
 epsilon = 1e-05
+MESH = pl.DeviceIdType.MESH
 
 
 def layer_norm(values, gain, shift):
@@ -106,6 +111,247 @@
     return lax.all_to_all(columns, "row", split_axis=0, concat_axis=1, tiled=True)
 
 
+def fused_kernel(
+    n,
+    align_ref,
+    pair_ref,
+    gain_ref,
+    offset_ref,
+    left_w_ref,
+    right_w_ref,
+    outer_w_ref,
+    outer_b_ref,
+    pair_gain_ref,
+    pair_shift_ref,
+    up_ref,
+    up_b_ref,
+    down_ref,
+    down_b_ref,
+    out_ref,
+    norm_s,
+    left_s,
+    right_s,
+    right_send,
+    left_all,
+    right_all,
+    pair_all,
+    pair_f,
+    outer_s,
+    outer_wt,
+    own_sem,
+    left_send_sem,
+    left_sem,
+    right_send_sem,
+    right_sem,
+    pair_send_sem,
+    pair_sem,
+):
+    me = lax.axis_index("row")
+    seqs, residues, channels = align_ref.shape
+    proj = left_w_ref.shape[1]
+    own = residues // n
+    lanes = 128
+    fold = lanes // proj
+    groups = own // fold
+    width = outer_w_ref.shape[1]
+    f32, bf16 = jnp.float32, jnp.bfloat16
+
+    barrier = pltpu.get_barrier_semaphore()
+    for k in range(1, n):
+        pl.semaphore_signal(barrier, inc=1, device_id={"row": lax.rem(me + k, n)}, device_id_type=MESH)
+
+    def remote(src, dst, send, recv, device):
+        return pltpu.make_async_remote_copy(
+            src_ref=src, dst_ref=dst, send_sem=send, recv_sem=recv,
+            device_id={"row": device}, device_id_type=MESH,
+        )
+
+    def row(ref):
+        return ref[...].reshape(1, ref.shape[0])
+
+    gain, offset = row(gain_ref), row(offset_ref)
+    for s in range(seqs):
+        normed = layer_norm(align_ref[s], gain, offset)
+        for h in range(channels // lanes):
+            norm_s[h, pl.ds(s * residues, residues), :] = normed[:, h * lanes : (h + 1) * lanes]
+        left = lax.dot_general(
+            left_w_ref[...], normed.astype(bf16), (((0,), (1,)), ((), ())), preferred_element_type=f32
+        )
+        left_s[pl.ds(s, proj, stride=seqs), :] = left
+    left_all[me] = left_s[...].reshape(proj, seqs, residues).astype(bf16)
+    parts = []
+    rows = seqs * residues // fold
+    for q in range(fold):
+        part = jnp.concatenate(
+            [norm_s[h, pl.ds(q, rows, stride=fold), :] for h in range(channels // lanes)], axis=1
+        ).astype(bf16)
+        parts.append(jnp.dot(part, right_w_ref[...], preferred_element_type=f32))
+    right_s[...] = jnp.concatenate(parts, axis=1)
+    for g in range(residues // fold):
+        right_send[g] = right_s[pl.ds(g, seqs, stride=residues // fold), :].astype(bf16)
+
+    pl.semaphore_wait(barrier, n - 1)
+
+    near = me + 1 - 2 * lax.rem(me, 2)
+    across = me + 2 - 4 * lax.rem(me // 2, 2)
+    sends = []
+
+    def send_left(src, device):
+        copy = remote(
+            left_all.at[src], left_all.at[src], left_send_sem.at[len(sends)], left_sem.at[src], device
+        )
+        copy.start()
+        sends.append(copy)
+
+    def wait_left(src):
+        remote(left_all.at[src], left_all.at[src], left_send_sem.at[0], left_sem.at[src], me).wait_recv()
+
+    for k in range(1, n // 4):
+        send_left(me, lax.rem(me + 4 * k, n))
+    send_left(me, across)
+    send_left(me, near)
+    rights, pairs = [], []
+    for k in range(1, n):
+        peer = lax.rem(me + k, n)
+        copy = remote(
+            right_send.at[pl.ds(peer * groups, groups)], right_all.at[me],
+            right_send_sem.at[k], right_sem.at[me], peer,
+        )
+        copy.start()
+        rights.append(copy)
+    own_right = pltpu.make_async_copy(
+        right_send.at[pl.ds(me * groups, groups)], right_all.at[me], own_sem.at[0]
+    )
+    own_right.start()
+    for k in range(1, n):
+        peer = lax.rem(me + k, n)
+        copy = remote(pair_ref.at[:, peer], pair_all.at[me], pair_send_sem.at[k], pair_sem.at[me], peer)
+        copy.start()
+        pairs.append(copy)
+    own_pair = pltpu.make_async_copy(pair_ref.at[:, me], pair_all.at[me], own_sem.at[1])
+    own_pair.start()
+
+    outer_wt[...] = outer_w_ref[...].astype(f32).T.astype(bf16)
+
+    for k in range(1, n // 4):
+        src = lax.rem(me + 4 * k, n)
+        wait_left(src)
+        send_left(src, across)
+        send_left(src, near)
+    for k in range(n // 4):
+        src = lax.rem(across + 4 * k, n)
+        wait_left(src)
+        send_left(src, near)
+    own_right.wait()
+    for k in range(1, n):
+        src = lax.rem(me + k, n)
+        remote(right_all.at[src], right_all.at[src], right_send_sem.at[k], right_sem.at[src], me).wait_recv()
+    right = jnp.concatenate(
+        [right_all[:, g].reshape(n * seqs, lanes) for g in range(groups)], axis=1
+    )
+    right_t = right.astype(f32).T.astype(bf16)
+    for k in range(n // 4):
+        for start in (near, near + across - me):
+            wait_left(lax.rem(start + 4 * k, n))
+
+    scale = 1.0 / (n * seqs)
+    for c in range(0, proj, 2):
+        both = jnp.concatenate(
+            [left_all[:, c + d].reshape(n * seqs, residues) for d in range(2)], axis=1
+        )
+        outer = (jnp.dot(right_t, both, preferred_element_type=f32) * scale).astype(bf16)
+        for d in range(2):
+            for j in range(own):
+                outer_s[(c + d) * proj : (c + d + 1) * proj, j * residues : (j + 1) * residues] = outer[
+                    j * proj : (j + 1) * proj, d * residues : (d + 1) * residues
+                ]
+
+    own_pair.wait()
+    for k in range(1, n):
+        src = lax.rem(me + k, n)
+        remote(pair_all.at[src], pair_all.at[src], pair_send_sem.at[k], pair_sem.at[src], me).wait_recv()
+    pair_f[...] = pair_all[...].astype(f32).reshape(pair_f.shape)
+
+    for j in range(0, own, 2):
+        summed_t = jnp.dot(
+            outer_wt[...], outer_s[:, j * residues : (j + 2) * residues], preferred_element_type=f32
+        )
+        for d in range(2):
+            summed = (
+                summed_t[:, d * residues : (d + 1) * residues].T
+                + pair_f[pl.ds(j + d, residues, stride=own), :]
+                + row(outer_b_ref)
+            )
+            normed = layer_norm(summed, row(pair_gain_ref), row(pair_shift_ref)).astype(bf16)
+            hidden = jax.nn.relu(
+                jnp.dot(normed, up_ref[...], preferred_element_type=f32) + row(up_b_ref)
+            ).astype(bf16)
+            result = summed + jnp.dot(hidden, down_ref[...], preferred_element_type=f32) + row(down_b_ref)
+            out_ref[j + d] = result.astype(bf16)
+
+    for copy in sends + rights + pairs:
+        copy.wait_send()
+
+
+def fused(n, alignment, pair_rep, *params):
+    seqs, residues, channels = alignment.shape
+    own = pair_rep.shape[0]
+    width = pair_rep.shape[2]
+    proj = params[2].shape[1]
+    lanes = 128
+    groups = own * proj // lanes
+    f32, bf16 = jnp.float32, jnp.bfloat16
+    vmem = pl.BlockSpec(memory_space=pltpu.VMEM)
+    return pl.pallas_call(
+        functools.partial(fused_kernel, n),
+        out_shape=jax.ShapeDtypeStruct((own, residues, width), bf16),
+        in_specs=[vmem, pl.BlockSpec(memory_space=pl.ANY)] + [vmem] * len(params),
+        out_specs=vmem,
+        scratch_shapes=[
+            pltpu.VMEM((channels // lanes, seqs * residues, lanes), f32),
+            pltpu.VMEM((proj * seqs, residues), f32),
+            pltpu.VMEM((seqs * residues * proj // lanes, lanes), f32),
+            pltpu.VMEM((residues * proj // lanes, seqs, lanes), bf16),
+            pltpu.VMEM((n, proj, seqs, residues), bf16),
+            pltpu.VMEM((n, groups, seqs, lanes), bf16),
+            pltpu.VMEM((n, own, own, width), bf16),
+            pltpu.VMEM((residues * own, width), f32),
+            pltpu.VMEM((proj * proj, own * residues), bf16),
+            pltpu.VMEM((width, proj * proj), bf16),
+            pltpu.SemaphoreType.DMA((2,)),
+            pltpu.SemaphoreType.DMA((n,)),
+            pltpu.SemaphoreType.DMA((n,)),
+            pltpu.SemaphoreType.DMA((n,)),
+            pltpu.SemaphoreType.DMA((n,)),
+            pltpu.SemaphoreType.DMA((n,)),
+            pltpu.SemaphoreType.DMA((n,)),
+        ],
+        compiler_params=pltpu.CompilerParams(collective_id=0, has_side_effects=True),
+    )(alignment, pair_rep.reshape(own, n, residues // n, width), *params)
+
+
+def fits(n, alignment, pair_rep, left_w):
+    seqs, residues = alignment.shape[:2]
+    own, width = pair_rep.shape[0], pair_rep.shape[2]
+    proj = left_w.shape[1]
+    return (
+        n % 4 == 0
+        and seqs == 8
+        and residues == 128
+        and width == 128
+        and own == 8
+        and alignment.shape[2] % 128 == 0
+        and proj % 32 == 0
+        and 128 % proj == 0
+    )
+
+
+def dispatch(n, *args):
+    if fits(n, args[0], args[1], args[4]):
+        return fused(n, *args)
+    return shards(*args)
+
+
 def solution(mesh):
     placed = (
         P(("group", "row"), None, None),
@@ -124,7 +370,7 @@
         P(),
     )
     return jax.shard_map(
-        shards,
+        functools.partial(dispatch, mesh.shape["row"]),
         mesh=mesh,
         in_specs=placed,
         out_specs=P(("group", "row"), None, None),

time: 89.1 us -> 32.8 us (0.37)
  the two profiles are of different devices: /device:TPU:0 before, /device:TPU:15 now
where the time goes in v1:
time: 32.8 us; the launch traced here: 32.5 us
  Pallas kernels  28.6 us (87%)
  local copies, waits for them, and re-layouts  3.86 us (12%)
    pallas_call x1, Pallas kernels, fused(): pl.pallas_call(functools.partial(fused_kernel, n), out_shape=jax.ShapeDty...  28.6 us
    unnamed x5, local copies, waits for them, and re-layouts  3.86 us

profile of v1, /device:TPU:15, one launch (start us, length us, event | category | flops | bytes accessed | tf_op | source)
XLA Modules:
  0.0 32.5 jit_solution(10362755487693411932)
XLA Ops:
  0.0 0.0 copy-start
  0.0 1.5 %copy.15.left_w_ref = bf16[256,32]{1,0:T(8,128)(2,1)} copy(bf16[256,32]{0,1:T(8,128)(2,1)} %param.18) | data formatting | bytes 32768 | tf_op args[4]
  1.5 0.0 copy-done
  1.5 0.7 %copy.16.right_w_ref = bf16[256,32]{1,0:T(8,128)(2,1)} copy(bf16[256,32]{0,1:T(8,128)(2,1)S(1)} %copy-done) | data formatting | bytes 32768 | tf_op args[5]
  2.2 28.6 %shard_map.136 = bf16[8,128,128]{2,1,0:T(8,128)(2,1)} custom-call(bf16[8,128,256]{2,1,0:T(8,128)(2,1)} %align_ref.1, bf16[8,16,8,128]{3,2,1,0:T(8,128)(2,1)} %bitcast.1, f32[256]{0:T(256)} %gain_ref.1, f32[256]{0:T(256)} %offset_ref.1, bf16[256,32]{1,0:T(8,128)(2,1)} %copy.15.left_w_ref, bf16[256,32]{1,0:T(8,128)(2,1)} %copy.16.right_w_ref, ...), custom_call_target="tpu_custom_call" | custom-call | tf_op jit(solution)/shard_map/pallas_call | solution.py:305
  30.8 1.7 %copy.18 = bf16[8,128,128]{2,1,0:T(8,128)(2,1)} copy(bf16[8,128,128]{2,1,0:T(8,128)(2,1)} %shard_map.136) | data formatting | bytes 524288
Async XLA Ops:
  0.0 1.5 %copy-start = (bf16[256,32]{0,1:T(8,128)(2,1)S(1)}, bf16[256,32]{0,1:T(8,128)(2,1)}, u32[]{:S(2)}) copy-start(bf16[256,32]{0,1:T(8,128)(2,1)} %param.19) | copy-start | bytes 49156
